TPU v7x, 32 devices: a whole 2x2x4 slice. The times are simulated.
32 devices in a mesh: groups: 2 (over y), seq: 4 (over z), head: 4 (over x, core).
Axes of the slice: x: 2, y: 2, z: 4, core: 2. Of those that a mesh axis runs over, the one named last changes fastest.
Arguments:
- doc_start: int32 [1024], P(('groups', 'seq')), parts along dimension 0, may hold values from 0 to 511, as said below
- q_gdn: bfloat16 [1024, 2048], P(('groups', 'seq'), 'head'), parts along dimension 0, may hold values from -6 to 6
- k_gdn: bfloat16 [1024, 2048], P(('groups', 'seq'), 'head'), parts along dimension 0, may hold values from -6 to 6
- v_gdn: bfloat16 [1024, 4096], P(('groups', 'seq'), 'head'), parts along dimension 0, may hold values from -6 to 6
- z_gdn: bfloat16 [1024, 4096], P(('groups', 'seq'), 'head'), parts along dimension 0, may hold values from -6 to 6
- beta_logit: float32 [32, 1024], P('head', ('groups', 'seq')), parts along dimension 1, may hold values from -8 to 3
- log_decay: float32 [32, 1024], P('head', ('groups', 'seq')), parts along dimension 1, may hold values from -1 to 0
- norm_weight: float32 [128], replicated, may hold values from 0.1 to 1.9
- q_attn: bfloat16 [1024, 4096], P(('groups', 'seq'), 'head'), parts along dimension 0, may hold values from -6 to 6
- k_attn: bfloat16 [1024, 512], P(('groups', 'seq')), parts along dimension 0, may hold values from -6 to 6
- v_attn: bfloat16 [1024, 512], P(('groups', 'seq')), parts along dimension 0, may hold values from -6 to 6
- gate_attn: bfloat16 [1024, 4096], P(('groups', 'seq'), 'head'), parts along dimension 0, may hold values from -6 to 6
Outputs:
- gdn_out: bfloat16 [1024, 4096], P(('groups', 'seq'), 'head'), parts along dimension 0
- attn_out: bfloat16 [1024, 4096], P(('groups', 'seq'), 'head'), parts along dimension 0
There are 2 independent parts, one for each index of `groups`. A program takes and returns all parts, laid end to end along the dimension named above; an argument that names none is the same for every part. Nothing has to cross between parts.
Inputs may be any that keep to these rules, and one draw needn't show every extreme that they name: Nondecreasing; doc_start[i] <= i, with equality exactly at the first token of each of the 3 documents; the first document starts at 0.
All inputs are finite; a program needn't handle non-finite values.
Results may differ from a plain program's by a relative error of at most 0.0095.
Values may be sent and summed in bfloat16 or wider, within the bound.
A program may use at most 128 MiB of HBM per device.

v0:
```python
import jax
import jax.numpy as jnp
from jax import lax
from jax.sharding import PartitionSpec as P

DK = 128
DV = 128
QH = 16
KVH = 2
HD_A = 256
BLOCK = 64
HIGH = lax.Precision.HIGHEST


def shifted(shard, axis, by):
    length = lax.axis_size(axis)
    pairs = [(i, i + by) for i in range(length) if 0 <= i + by < length]
    return lax.ppermute(shard, axis, pairs)


def unit_rows(values):
    return values * lax.rsqrt(jnp.sum(values * values, axis=-1, keepdims=True) + 1e-06)


def blocked(values, count):
    length, heads, width = values.shape
    return values.reshape(count, length // count, heads, width).transpose(0, 2, 1, 3)


def block_terms(anchor, doc_block, query, keys, values, beta, log_gate):
    width = query.shape[1]
    running = jnp.cumsum(log_gate, axis=1)
    place = anchor + jnp.arange(width, dtype=jnp.int32)
    causal = place[None, :] <= place[:, None]
    same = causal & (doc_block[:, None] <= place[None, :])
    strict = same & (place[None, :] < place[:, None])
    spread = jnp.where(same[None], running[:, :, None] - running[:, None, :], 0.0)
    decay = jnp.where(same[None], jnp.exp(spread), 0.0)
    alive = (doc_block < anchor).astype(jnp.float32)
    entry = jnp.exp(running) * alive[None, :]
    gram = jnp.einsum("hik,hjk->hij", keys, keys, precision=HIGH)
    lower_part = jnp.where(strict[None], decay * gram, 0.0)
    system = jnp.eye(width, dtype=jnp.float32)[None] + beta[:, :, None] * lower_part
    right = jnp.concatenate([beta[:, :, None] * values, (beta * entry)[:, :, None] * keys], axis=2)
    solved = lax.linalg.triangular_solve(
        system, right, left_side=True, lower=True, unit_diagonal=True
    )
    fresh = solved[:, :, : values.shape[2]]
    erased = solved[:, :, values.shape[2] :]
    scores = jnp.einsum("hik,hjk->hij", query, keys, precision=HIGH) * decay
    local_out = jnp.einsum("hij,hjv->hiv", scores, fresh, precision=HIGH)
    reach = entry[:, :, None] * query - jnp.einsum("hij,hjk->hik", scores, erased, precision=HIGH)
    tail_keys = decay[:, -1, :, None] * keys
    identity = jnp.eye(keys.shape[2], dtype=jnp.float32)
    carry_map = entry[:, -1, None, None] * identity[None] - jnp.einsum(
        "hjk,hjl->hkl", erased, tail_keys, precision=HIGH
    )
    carry_add = jnp.einsum("hjv,hjk->hvk", fresh, tail_keys, precision=HIGH)
    return (local_out, reach, carry_map, carry_add)


def compose(earlier, later):
    joined_map = jnp.einsum("hkl,hlm->hkm", earlier[0], later[0], precision=HIGH)
    joined_add = jnp.einsum("hvl,hlm->hvm", earlier[1], later[0], precision=HIGH) + later[1]
    return (joined_map, joined_add)


def entering_state(device_map, device_add):

    def relay(turn, pair):
        incoming, state = pair
        incoming = shifted(state.astype(jnp.bfloat16), "seq", 1).astype(state.dtype)
        state = jnp.einsum("hvk,hkl->hvl", incoming, device_map, precision=HIGH) + device_add
        return (incoming, state)

    start_state, _ = lax.fori_loop(
        0, lax.axis_size("seq") - 1, relay, (jnp.zeros_like(device_add), device_add)
    )
    return start_state


def delta_layer(doc_start, q_gdn, k_gdn, v_gdn, z_gdn, beta_logit, log_decay, norm_weight, anchor):
    length = q_gdn.shape[0]
    key_heads = q_gdn.shape[1] // DK
    value_heads = v_gdn.shape[1] // DV
    repeat = value_heads // key_heads
    count = length // BLOCK
    query = jnp.repeat(
        unit_rows(q_gdn.astype(jnp.float32).reshape(length, key_heads, DK)), repeat, axis=1
    )
    keys = jnp.repeat(
        unit_rows(k_gdn.astype(jnp.float32).reshape(length, key_heads, DK)), repeat, axis=1
    )
    values = v_gdn.astype(jnp.float32).reshape(length, value_heads, DV)
    beta = jax.nn.sigmoid(beta_logit).reshape(value_heads, count, BLOCK).transpose(1, 0, 2)
    log_gate = log_decay.reshape(value_heads, count, BLOCK).transpose(1, 0, 2)
    docs = doc_start.reshape(count, BLOCK)
    anchors = anchor + BLOCK * jnp.arange(count, dtype=jnp.int32)
    identity = jnp.broadcast_to(jnp.eye(DK, dtype=jnp.float32), (value_heads, DK, DK))

    def sweep(totals, inputs):
        total_map, total_add = totals
        block_anchor, doc_block, q_block, k_block, v_block, b_block, g_block = inputs
        local_out, reach, carry_map, carry_add = block_terms(
            block_anchor, doc_block, q_block, k_block, v_block, b_block, g_block
        )
        joined = compose((total_map, total_add), (carry_map, carry_add))
        return (joined, (local_out, reach, total_map, total_add))

    start_totals = (identity, jnp.zeros((value_heads, DV, DK), jnp.float32))
    scanned = (
        anchors,
        docs,
        blocked(query, count),
        blocked(keys, count),
        blocked(values, count),
        beta,
        log_gate,
    )
    (device_map, device_add), (local_out, reach, prefix_map, prefix_add) = lax.scan(
        sweep, start_totals, scanned
    )
    start_state = entering_state(device_map, device_add)
    block_state = jnp.einsum("hvk,chkl->chvl", start_state, prefix_map, precision=HIGH) + prefix_add
    mixed = local_out + jnp.einsum("chik,chvk->chiv", reach, block_state, precision=HIGH)
    mixed = mixed.transpose(0, 2, 1, 3).reshape(length, value_heads, DV)
    gate = z_gdn.astype(jnp.float32).reshape(length, value_heads, DV)
    factor = lax.rsqrt(jnp.mean(mixed * mixed, axis=-1, keepdims=True) + 1e-06)
    normed = mixed * factor * norm_weight * jax.nn.silu(gate)
    return normed.reshape(length, value_heads * DV).astype(jnp.bfloat16)


def attend(doc_start, q_attn, k_attn, v_attn, gate_attn, anchor):
    length = q_attn.shape[0]
    local_heads = q_attn.shape[1] // HD_A
    group = QH // KVH
    shards_seen = lax.axis_size("seq") // 2 + 1
    window_size = shards_seen * length
    kv_head = lax.axis_index("head") * local_heads // group
    keys_own = lax.dynamic_slice_in_dim(k_attn, kv_head * HD_A, HD_A, 1)
    values_own = lax.dynamic_slice_in_dim(v_attn, kv_head * HD_A, HD_A, 1)
    query = q_attn.reshape(length, local_heads, HD_A)
    q_place = anchor + jnp.arange(length, dtype=jnp.int32)
    lower = jnp.maximum(doc_start, q_place - window_size + 1)
    lowest = jnp.min(lower)
    highest = anchor + length - 1
    factor = HD_A ** (-0.5)
    initial = (
        jnp.full((local_heads, length), -1e30, jnp.float32),
        jnp.zeros((local_heads, length), jnp.float32),
        jnp.zeros((local_heads, length, HD_A), jnp.float32),
    )
    key_piece = lax.all_gather(keys_own, "seq", axis=0, tiled=True)
    value_piece = lax.all_gather(values_own, "seq", axis=0, tiled=True)
    count = key_piece.shape[0]
    width = count
    while width > 1024 and width % 2 == 0:
        width = width // 2

    def one(index, inner):
        begin = index * width
        key_part = lax.dynamic_slice_in_dim(key_piece, begin, width, 0)
        value_part = lax.dynamic_slice_in_dim(value_piece, begin, width, 0)
        k_place = begin + jnp.arange(width, dtype=jnp.int32)

        def compute(state):
            peak, total, accum = state
            scores = (
                jnp.einsum("qhd,kd->hqk", query, key_part, preferred_element_type=jnp.float32)
                * factor
            )
            visible = (k_place[None, :] >= lower[:, None]) & (k_place[None, :] <= q_place[:, None])
            masked = jnp.where(visible[None], scores, -jnp.inf)
            new_peak = jnp.maximum(peak, jnp.max(masked, axis=-1))
            weights = jnp.exp(masked - new_peak[:, :, None])
            shrink = jnp.exp(peak - new_peak)
            total = total * shrink + jnp.sum(weights, axis=-1)
            update = jnp.einsum(
                "hqk,kd->hqd",
                weights.astype(jnp.bfloat16),
                value_part,
                preferred_element_type=jnp.float32,
            )
            accum = accum * shrink[:, :, None] + update
            return (new_peak, total, accum)

        def unchanged(state):
            return state

        busy = (begin <= highest) & (begin + width - 1 >= lowest)
        return lax.cond(busy, compute, unchanged, inner)

    peak, total, accum = lax.fori_loop(0, count // width, one, initial)
    mixed = (accum / total[:, :, None]).transpose(1, 0, 2).reshape(length, local_heads * HD_A)
    return (mixed * jax.nn.sigmoid(gate_attn.astype(jnp.float32))).astype(jnp.bfloat16)


def shards(
    doc_start,
    q_gdn,
    k_gdn,
    v_gdn,
    z_gdn,
    beta_logit,
    log_decay,
    norm_weight,
    q_attn,
    k_attn,
    v_attn,
    gate_attn,
):
    anchor = lax.axis_index("seq") * q_gdn.shape[0]
    gdn_out = delta_layer(
        doc_start, q_gdn, k_gdn, v_gdn, z_gdn, beta_logit, log_decay, norm_weight, anchor
    )
    attn_out = attend(doc_start, q_attn, k_attn, v_attn, gate_attn, anchor)
    return (gdn_out, attn_out)


def solution(mesh):
    return jax.shard_map(
        shards,
        mesh=mesh,
        in_specs=(
            P(("groups", "seq")),
            P(("groups", "seq"), "head"),
            P(("groups", "seq"), "head"),
            P(("groups", "seq"), "head"),
            P(("groups", "seq"), "head"),
            P("head", ("groups", "seq")),
            P("head", ("groups", "seq")),
            P(),
            P(("groups", "seq"), "head"),
            P(("groups", "seq"), None),
            P(("groups", "seq"), None),
            P(("groups", "seq"), "head"),
        ),
        out_specs=(P(("groups", "seq"), "head"), P(("groups", "seq"), "head")),
        check_vma=False,
    )
```

profile of v0, /device:TPU:0, one launch (start us, length us, event | category | flops | bytes accessed | tf_op | source)
XLA Modules:
  0.0 189.3 jit_solution(7092509554987152704)
XLA Ops:
  0.7 1.0 reshape.347
  3.7 0.9 copy-done.13
  7.8 105.6 %while.13 = (s32[]{:T(128)}, f32[8,128,128]{1,2,0:T(8,128)S(1)}, f32[8,128,128]{1,2,0:T(8,128)S(1)}, f32[2,8,64,128]{3,2,1,0:T(8,128)}, f32[2,8,64,128]{3,2,1,0:...) while((s32[]{:T(128)}, f32[8,128,128]{1,2,0:T(8,128)S(1)}, ...), condition=%wide.region_4.5_spmd.clone, body=%wide.region_2.4_spmd.clone.sunk | while | flops 907780864 | bytes 40192524 | solution.py:120
  10.1 39.3 %custom-call.11 = f32[8,1,64,64]{2,3,1,0:T(8,128)S(1)} custom-call(f32[8,1,64,64]{3,2,1,0:T(8,128)S(1)} %fusion.124), custom_call_target="InvertDiagBlocksLowerTriangular" | custom-call | tf_op jit(solution)/shard_map/while/body/eval_jaxpr/triangular_solve | solution.py:45
  50.3 1.0 constant_dynamic-slice_fusion.9
  52.4 1.1 convolution_subtract_fusion.3
  53.5 1.0 convolution_bitcast_fusion.7
  55.2 1.1 convolution_add_fusion.7
  56.3 1.0 convolution_bitcast_fusion.6
  62.9 39.3 %custom-call.11 = f32[8,1,64,64]{2,3,1,0:T(8,128)S(1)} custom-call(f32[8,1,64,64]{3,2,1,0:T(8,128)S(1)} %fusion.124), custom_call_target="InvertDiagBlocksLowerTriangular" | custom-call | tf_op jit(solution)/shard_map/while/body/eval_jaxpr/triangular_solve | solution.py:45
  103.1 1.0 constant_dynamic-slice_fusion.9
  105.2 1.1 convolution_subtract_fusion.3
  106.3 1.0 convolution_bitcast_fusion.7
  108.0 1.1 convolution_add_fusion.7
  109.1 1.0 convolution_bitcast_fusion.6
  114.6 34.6 %while.12 = (s32[]{:T(128)}, f32[8,128,128]{2,1,0:T(8,128)}, bf16[8,128,128]{2,1,0:T(8,128)(2,1)}, f32[8,128,128]{2,1,0:T(8,128)S(1)}, f32[8,128,128]{2,1,0:T(8,128)S(1)}, /*index=5*/s32[]{:T(128)}) while((s32[]{:T(128)}, f32[8,128,128]{2,1,0:T(8,128)}, bf16[8,128,128]{2,1,0:T(8,128)(2,1)}, f32[8,128,128]{2,1,0:T(8,128)S(1)}, ...), condition=%wide.region_6.7_spmd, body=%wide.region_5.6_spmd.sunk | while | flops 201719808 | bytes 3407981 | solution.py:76
  114.6 5.1 %collective-permute-start = (bf16[8,128,128]{2,1,0:T(8,128)(2,1)}, bf16[8,128,128]{2,1,0:T(8,128)(2,1)S(1)}, u32[]{:S(2)}, u32[]{:S(2)}) collective-permute-start(bf16[8,128,128]{2,1,0:T(8,128)(2,1)} %get-tuple-element.581), channel_id=1, source_target_pairs={{0,4},{4,8},{8,12},{1,5},{5,9},{9,13},{2,6},{6,10},{10,14},{3,7},{... | collective-permute-start | bytes 786440 | tf_op jit(solution)/shard_map/while/body/eval_jaxpr/ppermute | solution.py:18
  119.8 5.8 %collective-permute-done = bf16[8,128,128]{2,1,0:T(8,128)(2,1)S(1)} collective-permute-done((bf16[8,128,128]{2,1,0:T(8,128)(2,1)}, bf16[8,128,128]{2,1,0:T(8,128)(2,1)S(1)}, u32[]{:S(2)}, u32[]{:S(2)}) %collective-permute-start) | collective-permute-done | bytes 262176 | tf_op jit(solution)/shard_map/while/body/eval_jaxpr/ppermute | solution.py:18
  126.4 1.1 convolution_add_fusion.6
  127.5 4.3 %collective-permute-start = (bf16[8,128,128]{2,1,0:T(8,128)(2,1)}, bf16[8,128,128]{2,1,0:T(8,128)(2,1)S(1)}, u32[]{:S(2)}, u32[]{:S(2)}) collective-permute-start(bf16[8,128,128]{2,1,0:T(8,128)(2,1)} %get-tuple-element.581), channel_id=1, source_target_pairs={{0,4},{4,8},{8,12},{1,5},{5,9},{9,13},{2,6},{6,10},{10,14},{3,7},{... | collective-permute-start | bytes 786440 | tf_op jit(solution)/shard_map/while/body/eval_jaxpr/ppermute | solution.py:18
  131.8 5.0 %collective-permute-done = bf16[8,128,128]{2,1,0:T(8,128)(2,1)S(1)} collective-permute-done((bf16[8,128,128]{2,1,0:T(8,128)(2,1)}, bf16[8,128,128]{2,1,0:T(8,128)(2,1)S(1)}, u32[]{:S(2)}, u32[]{:S(2)}) %collective-permute-start) | collective-permute-done | bytes 262176 | tf_op jit(solution)/shard_map/while/body/eval_jaxpr/ppermute | solution.py:18
  137.7 1.1 convolution_add_fusion.6
  138.8 4.3 %collective-permute-start = (bf16[8,128,128]{2,1,0:T(8,128)(2,1)}, bf16[8,128,128]{2,1,0:T(8,128)(2,1)S(1)}, u32[]{:S(2)}, u32[]{:S(2)}) collective-permute-start(bf16[8,128,128]{2,1,0:T(8,128)(2,1)} %get-tuple-element.581), channel_id=1, source_target_pairs={{0,4},{4,8},{8,12},{1,5},{5,9},{9,13},{2,6},{6,10},{10,14},{3,7},{... | collective-permute-start | bytes 786440 | tf_op jit(solution)/shard_map/while/body/eval_jaxpr/ppermute | solution.py:18
  143.1 4.2 %collective-permute-done = bf16[8,128,128]{2,1,0:T(8,128)(2,1)S(1)} collective-permute-done((bf16[8,128,128]{2,1,0:T(8,128)(2,1)}, bf16[8,128,128]{2,1,0:T(8,128)(2,1)S(1)}, u32[]{:S(2)}, u32[]{:S(2)}) %collective-permute-start) | collective-permute-done | bytes 262176 | tf_op jit(solution)/shard_map/while/body/eval_jaxpr/ppermute | solution.py:18
  148.1 1.1 convolution_add_fusion.6
  149.2 2.2 %fusion.53 = f32[2,8,128,128]{2,3,1,0:T(8,128)S(1)} fusion(f32[2,8,128,128]{2,3,1,0:T(8,128)S(1)} %copy-done.6, f32[2,8,128,128]{2,3,1,0:T(8,128)S(1)} %copy-done.3, f32[8,128,128]{2,1,0:T(8,128)} %get-tuple-element.215), kind=kOutput, calls=%fused_computation.91 | convolution fusion | flops 402915328 | bytes 3670016 | tf_op jit(solution)/shard_map/hvk,chkl->chvl/dot_general | solution.py:124
  151.4 1.1 multiply_reduce_fusion
  153.9 1.0 fusion.61
  154.9 15.6 %all_gather.6 = bf16[512,256]{1,0:T(8,128)(2,1)S(1)} all-gather(bf16[128,256]{1,0:T(8,128)(2,1)S(1)} %constant_dynamic-slice_fusion.5), channel_id=1, replica_groups=mesh['groups'=2,'seq'=4,'head'=4] {'seq'}, dimensions={0}, use_global_device_ids=true | all-gather | bytes 327680 | tf_op jit(solution)/shard_map/all_gather | solution.py:153
  170.5 14.0 %all_gather.7 = bf16[512,256]{1,0:T(8,128)(2,1)S(1)} all-gather(bf16[128,256]{1,0:T(8,128)(2,1)S(1)} %constant_dynamic-slice_fusion.4), channel_id=1, replica_groups=mesh['groups'=2,'seq'=4,'head'=4] {'seq'}, dimensions={0}, use_global_device_ids=true | all-gather | bytes 327680 | tf_op jit(solution)/shard_map/all_gather | solution.py:154
  186.1 1.2 conditional.1
  187.6 0.9 copy-done.15
  (159 shorter events, 29.1 us)
Async XLA Ops:
  0.6 154.2 %copy-start = (bf16[128,512]{1,0:T(8,128)(2,1)S(1)}, bf16[128,512]{1,0:T(8,128)(2,1)}, u32[]{:S(2)}) copy-start(bf16[128,512]{1,0:T(8,128)(2,1)} %param.27) | copy-start | bytes 393220
  2.2 0.9 copy-start.16
  3.6 1.0 copy-start.13
  5.6 0.7 copy-start.19
  6.3 0.7 copy-start.18
  53.5 1.2 copy-start.1
  53.5 1.5 copy-start.4
  55.1 2.2 %copy-start.2 = (f32[2,8,128,128]{2,3,1,0:T(8,128)}, f32[2,8,128,128]{2,3,1,0:T(8,128)S(1)}, u32[]{:S(2)}) copy-start(f32[2,8,128,128]{2,3,1,0:T(8,128)S(1)} %get-tuple-element.561) | copy-start | bytes 3145732 | tf_op jit(solution)/shard_map/while
  55.2 2.2 %copy-start.5 = (f32[2,8,128,128]{2,3,1,0:T(8,128)}, f32[2,8,128,128]{2,3,1,0:T(8,128)S(1)}, u32[]{:S(2)}) copy-start(f32[2,8,128,128]{2,3,1,0:T(8,128)S(1)} %get-tuple-element.562) | copy-start | bytes 3145732 | tf_op jit(solution)/shard_map/while
  57.3 1.0 copy-start.10
  58.4 1.0 copy-start.7
  58.8 1.0 copy-start.11
  59.8 0.8 copy-start.8
  106.3 1.2 copy-start.1
  106.3 1.5 copy-start.4
  108.0 2.2 %copy-start.2 = (f32[2,8,128,128]{2,3,1,0:T(8,128)}, f32[2,8,128,128]{2,3,1,0:T(8,128)S(1)}, u32[]{:S(2)}) copy-start(f32[2,8,128,128]{2,3,1,0:T(8,128)S(1)} %get-tuple-element.561) | copy-start | bytes 3145732 | tf_op jit(solution)/shard_map/while
  108.0 2.2 %copy-start.5 = (f32[2,8,128,128]{2,3,1,0:T(8,128)}, f32[2,8,128,128]{2,3,1,0:T(8,128)S(1)}, u32[]{:S(2)}) copy-start(f32[2,8,128,128]{2,3,1,0:T(8,128)S(1)} %get-tuple-element.562) | copy-start | bytes 3145732 | tf_op jit(solution)/shard_map/while
  110.2 1.0 copy-start.10
  111.2 1.0 copy-start.7
  111.6 1.0 copy-start.11
  112.6 0.8 copy-start.8
  114.6 34.6 %copy-start.3 = (f32[2,8,128,128]{2,3,1,0:T(8,128)S(1)}, f32[2,8,128,128]{2,3,1,0:T(8,128)}, u32[]{:S(2)}) copy-start(f32[2,8,128,128]{2,3,1,0:T(8,128)} %get-tuple-element.212) | copy-start | bytes 3145732
  114.6 34.6 %copy-start.6 = (f32[2,8,128,128]{2,3,1,0:T(8,128)S(1)}, f32[2,8,128,128]{2,3,1,0:T(8,128)}, u32[]{:S(2)}) copy-start(f32[2,8,128,128]{2,3,1,0:T(8,128)} %get-tuple-element.216) | copy-start | bytes 3145732
  114.6 11.0 %collective-permute-start = (bf16[8,128,128]{2,1,0:T(8,128)(2,1)}, bf16[8,128,128]{2,1,0:T(8,128)(2,1)S(1)}, u32[]{:S(2)}, u32[]{:S(2)}) collective-permute-start(bf16[8,128,128]{2,1,0:T(8,128)(2,1)} %get-tuple-element.581), channel_id=1, source_target_pairs={{0,4},{4,8},{8,12},{1,5},{5,9},{9,13},{2,6},{6,10},{10,14},{3,7},{... | collective-permute-start | bytes 786440 | tf_op jit(solution)/shard_map/while/body/eval_jaxpr/ppermute | solution.py:18
  127.5 9.3 %collective-permute-start = (bf16[8,128,128]{2,1,0:T(8,128)(2,1)}, bf16[8,128,128]{2,1,0:T(8,128)(2,1)S(1)}, u32[]{:S(2)}, u32[]{:S(2)}) collective-permute-start(bf16[8,128,128]{2,1,0:T(8,128)(2,1)} %get-tuple-element.581), channel_id=1, source_target_pairs={{0,4},{4,8},{8,12},{1,5},{5,9},{9,13},{2,6},{6,10},{10,14},{3,7},{... | collective-permute-start | bytes 786440 | tf_op jit(solution)/shard_map/while/body/eval_jaxpr/ppermute | solution.py:18
  138.8 8.5 %collective-permute-start = (bf16[8,128,128]{2,1,0:T(8,128)(2,1)}, bf16[8,128,128]{2,1,0:T(8,128)(2,1)S(1)}, u32[]{:S(2)}, u32[]{:S(2)}) collective-permute-start(bf16[8,128,128]{2,1,0:T(8,128)(2,1)} %get-tuple-element.581), channel_id=1, source_target_pairs={{0,4},{4,8},{8,12},{1,5},{5,9},{9,13},{2,6},{6,10},{10,14},{3,7},{... | collective-permute-start | bytes 786440 | tf_op jit(solution)/shard_map/while/body/eval_jaxpr/ppermute | solution.py:18
  149.2 2.2 %copy-start.9 = (f32[2,8,64,128]{3,2,1,0:T(8,128)S(1)}, f32[2,8,64,128]{3,2,1,0:T(8,128)}, u32[]{:S(2)}) copy-start(f32[2,8,64,128]{3,2,1,0:T(8,128)} %get-tuple-element.210) | copy-start | bytes 1572868
  149.2 2.2 %copy-start.12 = (f32[2,8,64,128]{3,2,1,0:T(8,128)S(1)}, f32[2,8,64,128]{3,2,1,0:T(8,128)}, u32[]{:S(2)}) copy-start(f32[2,8,64,128]{3,2,1,0:T(8,128)} %get-tuple-element.211) | copy-start | bytes 1572868
  152.9 1.0 copy-start.14
  154.9 15.6 %copy-start.17 = (bf16[128,512]{1,0:T(8,128)(2,1)S(1)}, bf16[128,512]{1,0:T(8,128)(2,1)}, u32[]{:S(2)}) copy-start(bf16[128,512]{1,0:T(8,128)(2,1)} %param.28) | copy-start | bytes 393220
  185.2 0.9 copy-start.22
  187.5 1.0 copy-start.15
  (2 other events, 1.3 us)
where the time goes:
time: 190 us; the launch traced here: 189 us
  other arithmetic  90.3 us (48%)
  blocking collectives  29.7 us (16%)
  matrix products  21.1 us (11%)
  local copies, waits for them, and re-layouts  17.3 us (9%)
  waiting for transfers between devices  15 us (8%)
  starting transfers between devices  13.7 us (7%)
    another operation x6, other arithmetic, block_terms(): lax.linalg.triangular_solve(system, right, left_side=True, lower=True, un...  78.8 us
    all_gather x1, blocking collectives, attend(): key_piece = lax.all_gather(keys_own, 'seq', axis=0, tiled=True)  15.6 us
    ppermute x3, waiting for transfers between devices, shifted(): return lax.ppermute(shard, axis, pairs)  15 us
    all_gather x1, blocking collectives, attend(): value_piece = lax.all_gather(values_own, 'seq', axis=0, tiled=True)  14 us
    ppermute x3, starting transfers between devices, shifted(): return lax.ppermute(shard, axis, pairs)  13.7 us
    unnamed x31, local copies, waits for them, and re-layouts  5.57 us
    while x34, local copies, waits for them, and re-layouts  4.8 us
  transfers between devices with their start and end apart: 3, of which 3 were waited for; matrix products, arithmetic and copies ran while one was open for 0% of the time, Pallas kernels for 0%

commit v1 on v0

--- a/solution.py
+++ b/solution.py
@@ -150,7 +150,25 @@
         jnp.zeros((local_heads, length), jnp.float32),
         jnp.zeros((local_heads, length, HD_A), jnp.float32),
     )
-    key_piece = lax.all_gather(keys_own, "seq", axis=0, tiled=True)
+    count_2, mine, rows = (lax.axis_size("seq"), lax.axis_index("seq"), keys_own.shape[0])
+    route = [(i_2, (i_2 + 1) % count_2) for i_2 in range(count_2)]
+    backward = [(i_2, (i_2 - 1) % count_2) for i_2 in range(count_2)]
+    key_piece = jnp.zeros(
+        (*keys_own.shape[:0], count_2 * rows, *keys_own.shape[0 + 1 :]), keys_own.dtype
+    )
+    key_piece = lax.dynamic_update_slice_in_dim(key_piece, keys_own, mine * rows, axis=0)
+    from_left = from_right = keys_own
+    halfway = count_2 // 2
+    for step in range(1, halfway + 1):
+        from_left = lax.ppermute(from_left, "seq", route)
+        key_piece = lax.dynamic_update_slice_in_dim(
+            key_piece, from_left, (mine - step) % count_2 * rows, axis=0
+        )
+        if step < count_2 - halfway:
+            from_right = lax.ppermute(from_right, "seq", backward)
+            key_piece = lax.dynamic_update_slice_in_dim(
+                key_piece, from_right, (mine + step) % count_2 * rows, axis=0
+            )
     value_piece = lax.all_gather(values_own, "seq", axis=0, tiled=True)
     count = key_piece.shape[0]
     width = count

time: 190 us -> 186 us (0.979)
  blocking collectives: 29.7 us -> 14.1 us
  starting transfers between devices: 13.7 us -> 18.5 us
  local copies, waits for them, and re-layouts: 17.3 us -> 21.1 us
  matrix products: 21.1 us -> 24.7 us
  waiting for transfers between devices: 15 us -> 12.9 us
    all_gather x1 -> x0, blocking collectives: 15.6 us -> none  [attend(): key_piece = lax.all_gather(keys_own, 'seq', axis=0, tiled=True)]
    ppermute x0 -> x3, starting transfers between devices: none -> 7.61 us  [the longest x2 5.59 us: attend(): from_left = lax.ppermute(from_left, 'seq', route)]
    dynamic_update_slice x0 -> x4, local copies, waits for them, and re-layouts: none -> 4.44 us  [the longest x2 1.83 us: attend(): lax.dynamic_update_slice_in_dim(key_piece, from_left, (mine - step) % cou...]
    ppermute x3, starting transfers between devices: 13.7 us -> 10.9 us  [shifted(): return lax.ppermute(shard, axis, pairs)]
    dot_general x3, matrix products: 3.32 us -> 1.2 us  [relay(): jnp.einsum('hvk,hkl->hvl', incoming, device_map, precision=HIGH)]
    ppermute x3, waiting for transfers between devices: 15 us -> 12.9 us  [shifted(): return lax.ppermute(shard, axis, pairs)]
    while x34 -> x50, local copies, waits for them, and re-layouts: 4.8 us -> 3.34 us
  transfers between devices with their start and end apart: 3 -> 6, of which waited for: 3 -> 3; matrix products, arithmetic and copies ran while one was open for 0% -> 65% of each run, Pallas kernels for 0% -> 0%
where the time goes in v1:
time: 186 us; the launch traced here: 185 us
  other arithmetic  91.5 us (49%)
  matrix products  24.7 us (13%)
  local copies, waits for them, and re-layouts  21.1 us (11%)
  starting transfers between devices  18.5 us (10%)
  blocking collectives  14.1 us (8%)
  waiting for transfers between devices  12.9 us (7%)
    another operation x6, other arithmetic, block_terms(): lax.linalg.triangular_solve(system, right, left_side=True, lower=True, un...  80.3 us
    all_gather x1, blocking collectives, attend(): value_piece = lax.all_gather(values_own, 'seq', axis=0, tiled=True)  14.1 us
    ppermute x3, waiting for transfers between devices, shifted(): return lax.ppermute(shard, axis, pairs)  12.9 us
    ppermute x3, starting transfers between devices, shifted(): return lax.ppermute(shard, axis, pairs)  10.9 us
    unnamed x31, local copies, waits for them, and re-layouts  7.29 us
    ppermute x2, starting transfers between devices, attend(): from_left = lax.ppermute(from_left, 'seq', route)  5.59 us
  transfers between devices with their start and end apart: 6, of which 3 were waited for; matrix products, arithmetic and copies ran while one was open for 65% of the time, Pallas kernels for 0%

profile of v1, /device:TPU:0, one launch (start us, length us, event | category | flops | bytes accessed | tf_op | source)
XLA Modules:
  0.0 185.2 jit_solution(10616960518645199346)
XLA Ops:
  2.2 3.1 %collective-permute-start.1 = (bf16[128,256]{1,0:T(8,128)(2,1)}, bf16[128,256]{1,0:T(8,128)(2,1)}, u32[]{:S(2)}, u32[]{:S(2)}) collective-permute-start(bf16[128,256]{1,0:T(8,128)(2,1)} %constant_dynamic-slice_fusion.5), channel_id=1, source_target_pairs={{0,4},{4,8},{8,12},{12,0},{1,5},{5,9},{9,13},{13,1},{2,6},{6,10},{... | collective-permute-start | bytes 196616 | tf_op jit(solution)/shard_map/ppermute | solution.py:163
  5.2 2.0 %collective-permute-start.2 = (bf16[128,256]{1,0:T(8,128)(2,1)}, bf16[128,256]{1,0:T(8,128)(2,1)}, u32[]{:S(2)}, u32[]{:S(2)}) collective-permute-start(bf16[128,256]{1,0:T(8,128)(2,1)} %constant_dynamic-slice_fusion.5), channel_id=1, source_target_pairs={{0,12},{4,0},{8,4},{12,8},{1,13},{5,1},{9,5},{13,9},{2,14},{6,2},{... | collective-permute-start | bytes 196616 | tf_op jit(solution)/shard_map/ppermute | solution.py:168
  8.0 1.3 fusion.64
  14.6 109.3 %while.13 = (s32[]{:T(128)}, f32[8,128,128]{1,2,0:T(8,128)S(1)}, f32[8,128,128]{1,2,0:T(8,128)S(1)}, f32[2,8,64,128]{3,2,1,0:T(8,128)}, f32[2,8,64,128]{3,2,1,0:...) while((s32[]{:T(128)}, f32[8,128,128]{1,2,0:T(8,128)S(1)}, ...), condition=%wide.region_4.5_spmd.clone, body=%wide.region_2.4_spmd.clone.sunk | while | flops 907780864 | bytes 36036276 | solution.py:120
  17.5 1.3 fusion.124
  18.8 40.0 %custom-call.11 = f32[8,1,64,64]{2,3,1,0:T(8,128)S(1)} custom-call(f32[8,1,64,64]{3,2,1,0:T(8,128)} %fusion.124), custom_call_target="InvertDiagBlocksLowerTriangular" | custom-call | tf_op jit(solution)/shard_map/while/body/eval_jaxpr/triangular_solve | solution.py:45
  60.9 1.1 convolution_subtract_fusion.3
  63.7 1.1 convolution_add_fusion.7
  64.8 1.0 convolution_bitcast_fusion.6
  66.4 1.1 fusion.127
  67.5 1.1 fusion.126
  72.1 1.3 fusion.124
  73.4 40.0 %custom-call.11 = f32[8,1,64,64]{2,3,1,0:T(8,128)S(1)} custom-call(f32[8,1,64,64]{3,2,1,0:T(8,128)} %fusion.124), custom_call_target="InvertDiagBlocksLowerTriangular" | custom-call | tf_op jit(solution)/shard_map/while/body/eval_jaxpr/triangular_solve | solution.py:45
  115.5 1.1 convolution_subtract_fusion.3
  118.3 1.1 convolution_add_fusion.7
  121.0 1.1 fusion.127
  122.1 1.1 fusion.126
  124.3 27.6 %while.12 = (s32[]{:T(128)}, f32[8,128,128]{2,1,0:T(8,128)}, bf16[8,128,128]{2,1,0:T(8,128)(2,1)S(1)}, f32[8,128,128]{2,1,0:T(8,128)S(1)}, f32[8,128,128]{2,1,0:T(8,128)S(1)}, /*index=5*/s32[]{:T(128)}) while((s32[]{:T(128)}, f32[8,128,128]{2,1,0:T(8,128)}, bf16[8,128,128]{2,1,0:T(8,128)(2,1)S(1)}, f32[8,128,128]{2,1,0:T(8,128)S(1)}, ...), condition=%wide.region_6.7_spmd, body=%wide.region_5.6_spmd.sunk | while | flops 201719808 | bytes 3407981 | solution.py:76
  124.4 2.1 %collective-permute-start = (bf16[8,128,128]{2,1,0:T(8,128)(2,1)S(1)}, bf16[8,128,128]{2,1,0:T(8,128)(2,1)S(1)}, u32[]{:S(2)}, u32[]{:S(2)}) collective-permute-start(bf16[8,128,128]{2,1,0:T(8,128)(2,1)S(1)} %get-tuple-element.850), channel_id=1, source_target_pairs={{0,4},{4,8},{8,12},{1,5},{5,9},{9,13},{2,6},{6,10},{10,14},{3,7},{... | collective-permute-start | bytes 786440 | tf_op jit(solution)/shard_map/while/body/eval_jaxpr/ppermute | solution.py:18
  126.4 5.0 %collective-permute-done = bf16[8,128,128]{2,1,0:T(8,128)(2,1)S(1)} collective-permute-done((bf16[8,128,128]{2,1,0:T(8,128)(2,1)S(1)}, bf16[8,128,128]{2,1,0:T(8,128)(2,1)S(1)}, u32[]{:S(2)}, u32[]{:S(2)}) %collective-permute-start) | collective-permute-done | bytes 262176 | tf_op jit(solution)/shard_map/while/body/eval_jaxpr/ppermute | solution.py:18
  132.6 4.4 %collective-permute-start = (bf16[8,128,128]{2,1,0:T(8,128)(2,1)S(1)}, bf16[8,128,128]{2,1,0:T(8,128)(2,1)S(1)}, u32[]{:S(2)}, u32[]{:S(2)}) collective-permute-start(bf16[8,128,128]{2,1,0:T(8,128)(2,1)S(1)} %get-tuple-element.850), channel_id=1, source_target_pairs={{0,4},{4,8},{8,12},{1,5},{5,9},{9,13},{2,6},{6,10},{10,14},{3,7},{... | collective-permute-start | bytes 786440 | tf_op jit(solution)/shard_map/while/body/eval_jaxpr/ppermute | solution.py:18
  137.1 4.1 %collective-permute-done = bf16[8,128,128]{2,1,0:T(8,128)(2,1)S(1)} collective-permute-done((bf16[8,128,128]{2,1,0:T(8,128)(2,1)S(1)}, bf16[8,128,128]{2,1,0:T(8,128)(2,1)S(1)}, u32[]{:S(2)}, u32[]{:S(2)}) %collective-permute-start) | collective-permute-done | bytes 262176 | tf_op jit(solution)/shard_map/while/body/eval_jaxpr/ppermute | solution.py:18
  142.4 4.4 %collective-permute-start = (bf16[8,128,128]{2,1,0:T(8,128)(2,1)S(1)}, bf16[8,128,128]{2,1,0:T(8,128)(2,1)S(1)}, u32[]{:S(2)}, u32[]{:S(2)}) collective-permute-start(bf16[8,128,128]{2,1,0:T(8,128)(2,1)S(1)} %get-tuple-element.850), channel_id=1, source_target_pairs={{0,4},{4,8},{8,12},{1,5},{5,9},{9,13},{2,6},{6,10},{10,14},{3,7},{... | collective-permute-start | bytes 786440 | tf_op jit(solution)/shard_map/while/body/eval_jaxpr/ppermute | solution.py:18
  146.8 3.9 %collective-permute-done = bf16[8,128,128]{2,1,0:T(8,128)(2,1)S(1)} collective-permute-done((bf16[8,128,128]{2,1,0:T(8,128)(2,1)S(1)}, bf16[8,128,128]{2,1,0:T(8,128)(2,1)S(1)}, u32[]{:S(2)}, u32[]{:S(2)}) %collective-permute-start) | collective-permute-done | bytes 262176 | tf_op jit(solution)/shard_map/while/body/eval_jaxpr/ppermute | solution.py:18
  151.9 2.4 %fusion.53 = f32[2,8,128,128]{2,3,1,0:T(8,128)S(1)} fusion(f32[2,8,128,128]{2,3,1,0:T(8,128)} %get-tuple-element.319, f32[2,8,128,128]{2,3,1,0:T(8,128)S(1)} %copy-done.5, f32[8,128,128]{2,1,0:T(8,128)} %get-tuple-element.318), kind=kOutput, calls=%fused_computation.91 | convolution fusion | flops 402915328 | bytes 3670016 | tf_op jit(solution)/shard_map/hvk,chkl->chvl/dot_general | solution.py:124
  154.4 2.3 %multiply_reduce_fusion = (f32[2,64,8]{1,2,0:T(8,128)S(1)}, f32[2,64,8,128]{3,1,2,0:T(8,128)S(1)}) fusion(f32[2,8,64,128]{3,2,1,0:T(8,128)} %get-tuple-element.313, f32[2,8,64,128]{3,2,1,0:T(8,128)} %get-tuple-element.314, f32[2,8,128,128]{2,3,1,0:T(8,128)S(1)} %fusion.53), kind=kOutput, calls=%fused_computation.107 | convolution fusion | flops 201718784 | bytes 2625536 | tf_op jit(solution)/shard_map/chik,chvk->chiv/dot_general | solution.py:125
  160.2 2.5 %collective-permute-start.3 = (bf16[128,256]{1,0:T(8,128)(2,1)}, bf16[128,256]{1,0:T(8,128)(2,1)S(1)}, u32[]{:S(2)}, u32[]{:S(2)}) collective-permute-start(bf16[128,256]{1,0:T(8,128)(2,1)} %collective-permute-done.1), channel_id=1, source_target_pairs={{0,4},{4,8},{8,12},{12,0},{1,5},{5,9},{9,13},{13,1},{2,6},{6,10},{... | collective-permute-start | bytes 196616 | tf_op jit(solution)/shard_map/ppermute | solution.py:163
  162.8 14.1 %all_gather.3 = bf16[512,256]{1,0:T(8,128)(2,1)S(1)} all-gather(bf16[128,256]{1,0:T(8,128)(2,1)S(1)} %constant_dynamic-slice_fusion.4), channel_id=1, replica_groups=mesh['groups'=2,'seq'=4,'head'=4] {'seq'}, dimensions={0}, use_global_device_ids=true | all-gather | bytes 327680 | tf_op jit(solution)/shard_map/all_gather | solution.py:172
  177.5 5.8 %conditional.1 = ((f32[4,128]{1,0:T(4,128)S(1)}, f32[4,128,256]{2,1,0:T(8,128)S(1)})) conditional(s32[]{:T(128)} %convert_element_type.52, (f32[4,128]{1,0:T(4,128)S(1)}, f32[4,128,256]{2,1,0:T(8,128)S(1)}) %tuple.53, (s32[512]{0:T(512)S(1)}, s32[512]{0:T(512)S(1)}, s32[128]{0:T(128)S(1)}, s32[128]{0:T(128)S(1)}, s32[]{:T(128)}, ...), branch_computations={%region_9.10_spmd, %region_10.13_spmd.clone.clone} | conditional | flops 270730784 | bytes 5928351 | solution.py:209
  177.5 1.3 dynamic_update_slice.50
  178.8 1.2 dynamic_update_slice.51
  180.1 1.3 dynamic_update_slice.52
  (185 shorter events, 34.9 us)
Async XLA Ops:
  0.6 0.9 copy-start
  0.7 8.7 %copy-start.11 = (bf16[128,512]{1,0:T(8,128)(2,1)S(1)}, bf16[128,512]{1,0:T(8,128)(2,1)}, u32[]{:S(2)}) copy-start(bf16[128,512]{1,0:T(8,128)(2,1)} %param.20) | copy-start | bytes 393220
  2.2 158.1 %collective-permute-start.1 = (bf16[128,256]{1,0:T(8,128)(2,1)}, bf16[128,256]{1,0:T(8,128)(2,1)}, u32[]{:S(2)}, u32[]{:S(2)}) collective-permute-start(bf16[128,256]{1,0:T(8,128)(2,1)} %constant_dynamic-slice_fusion.5), channel_id=1, source_target_pairs={{0,4},{4,8},{8,12},{12,0},{1,5},{5,9},{9,13},{13,1},{2,6},{6,10},{... | collective-permute-start | bytes 196616 | tf_op jit(solution)/shard_map/ppermute | solution.py:163
  5.2 171.6 %collective-permute-start.2 = (bf16[128,256]{1,0:T(8,128)(2,1)}, bf16[128,256]{1,0:T(8,128)(2,1)}, u32[]{:S(2)}, u32[]{:S(2)}) collective-permute-start(bf16[128,256]{1,0:T(8,128)(2,1)} %constant_dynamic-slice_fusion.5), channel_id=1, source_target_pairs={{0,12},{4,0},{8,4},{12,8},{1,13},{5,1},{9,5},{13,9},{2,14},{6,2},{... | collective-permute-start | bytes 196616 | tf_op jit(solution)/shard_map/ppermute | solution.py:168
  9.9 0.9 copy-start.12
  11.3 1.0 copy-start.8
  14.6 1.8 copy-start.13
  14.6 44.2 %copy-start.16 = (s32[2,64]{1,0:T(2,128)}, s32[2,64]{1,0:T(2,128)S(1)}, u32[]{:S(2)}) copy-start(s32[2,64]{1,0:T(2,128)S(1)} %get-tuple-element.833) | copy-start | bytes 1540 | tf_op jit(solution)/shard_map/while
  14.7 45.0 %copy-start.1 = (f32[2,8,64,128]{3,1,2,0:T(8,128)}, f32[2,8,64,128]{3,1,2,0:T(8,128)S(1)}, u32[]{:S(2)}) copy-start(f32[2,8,64,128]{3,1,2,0:T(8,128)S(1)} %get-tuple-element.837) | copy-start | bytes 1572868 | tf_op jit(solution)/shard_map/while
  62.0 1.2 copy-start.3
  62.0 1.5 copy-start.6
  63.6 2.1 %copy-start.4 = (f32[2,8,128,128]{2,3,1,0:T(8,128)}, f32[2,8,128,128]{2,3,1,0:T(8,128)S(1)}, u32[]{:S(2)}) copy-start(f32[2,8,128,128]{2,3,1,0:T(8,128)S(1)} %get-tuple-element.830) | copy-start | bytes 3145732 | tf_op jit(solution)/shard_map/while
  63.6 2.1 %copy-start.7 = (f32[2,8,128,128]{2,3,1,0:T(8,128)}, f32[2,8,128,128]{2,3,1,0:T(8,128)S(1)}, u32[]{:S(2)}) copy-start(f32[2,8,128,128]{2,3,1,0:T(8,128)S(1)} %get-tuple-element.831) | copy-start | bytes 3145732 | tf_op jit(solution)/shard_map/while
  67.5 1.1 copy-start.2
  69.3 1.8 copy-start.13
  69.3 44.2 %copy-start.16 = (s32[2,64]{1,0:T(2,128)}, s32[2,64]{1,0:T(2,128)S(1)}, u32[]{:S(2)}) copy-start(s32[2,64]{1,0:T(2,128)S(1)} %get-tuple-element.833) | copy-start | bytes 1540 | tf_op jit(solution)/shard_map/while
  69.3 45.0 %copy-start.1 = (f32[2,8,64,128]{3,1,2,0:T(8,128)}, f32[2,8,64,128]{3,1,2,0:T(8,128)S(1)}, u32[]{:S(2)}) copy-start(f32[2,8,64,128]{3,1,2,0:T(8,128)S(1)} %get-tuple-element.837) | copy-start | bytes 1572868 | tf_op jit(solution)/shard_map/while
  116.6 1.2 copy-start.3
  116.6 1.5 copy-start.6
  118.3 2.1 %copy-start.4 = (f32[2,8,128,128]{2,3,1,0:T(8,128)}, f32[2,8,128,128]{2,3,1,0:T(8,128)S(1)}, u32[]{:S(2)}) copy-start(f32[2,8,128,128]{2,3,1,0:T(8,128)S(1)} %get-tuple-element.830) | copy-start | bytes 3145732 | tf_op jit(solution)/shard_map/while
  118.3 2.1 %copy-start.7 = (f32[2,8,128,128]{2,3,1,0:T(8,128)}, f32[2,8,128,128]{2,3,1,0:T(8,128)S(1)}, u32[]{:S(2)}) copy-start(f32[2,8,128,128]{2,3,1,0:T(8,128)S(1)} %get-tuple-element.831) | copy-start | bytes 3145732 | tf_op jit(solution)/shard_map/while
  122.1 1.1 copy-start.2
  123.2 0.7 copy-start.26
  124.3 27.6 %copy-start.5 = (f32[2,8,128,128]{2,3,1,0:T(8,128)S(1)}, f32[2,8,128,128]{2,3,1,0:T(8,128)}, u32[]{:S(2)}) copy-start(f32[2,8,128,128]{2,3,1,0:T(8,128)} %get-tuple-element.315) | copy-start | bytes 3145732
  124.4 7.0 %collective-permute-start = (bf16[8,128,128]{2,1,0:T(8,128)(2,1)S(1)}, bf16[8,128,128]{2,1,0:T(8,128)(2,1)S(1)}, u32[]{:S(2)}, u32[]{:S(2)}) collective-permute-start(bf16[8,128,128]{2,1,0:T(8,128)(2,1)S(1)} %get-tuple-element.850), channel_id=1, source_target_pairs={{0,4},{4,8},{8,12},{1,5},{5,9},{9,13},{2,6},{6,10},{10,14},{3,7},{... | collective-permute-start | bytes 786440 | tf_op jit(solution)/shard_map/while/body/eval_jaxpr/ppermute | solution.py:18
  132.6 8.5 %collective-permute-start = (bf16[8,128,128]{2,1,0:T(8,128)(2,1)S(1)}, bf16[8,128,128]{2,1,0:T(8,128)(2,1)S(1)}, u32[]{:S(2)}, u32[]{:S(2)}) collective-permute-start(bf16[8,128,128]{2,1,0:T(8,128)(2,1)S(1)} %get-tuple-element.850), channel_id=1, source_target_pairs={{0,4},{4,8},{8,12},{1,5},{5,9},{9,13},{2,6},{6,10},{10,14},{3,7},{... | collective-permute-start | bytes 786440 | tf_op jit(solution)/shard_map/while/body/eval_jaxpr/ppermute | solution.py:18
  142.4 8.3 %collective-permute-start = (bf16[8,128,128]{2,1,0:T(8,128)(2,1)S(1)}, bf16[8,128,128]{2,1,0:T(8,128)(2,1)S(1)}, u32[]{:S(2)}, u32[]{:S(2)}) collective-permute-start(bf16[8,128,128]{2,1,0:T(8,128)(2,1)S(1)} %get-tuple-element.850), channel_id=1, source_target_pairs={{0,4},{4,8},{8,12},{1,5},{5,9},{9,13},{2,6},{6,10},{10,14},{3,7},{... | collective-permute-start | bytes 786440 | tf_op jit(solution)/shard_map/while/body/eval_jaxpr/ppermute | solution.py:18
  158.3 1.0 copy-start.9
  159.2 1.0 copy-start.15
  160.2 16.6 %copy-start.24 = (bf16[128,1024]{1,0:T(8,128)(2,1)S(1)}, bf16[128,1024]{1,0:T(8,128)(2,1)}, u32[]{:S(2)}) copy-start(bf16[128,1024]{1,0:T(8,128)(2,1)} %param.26) | copy-start | bytes 786436
  160.2 16.6 %collective-permute-start.3 = (bf16[128,256]{1,0:T(8,128)(2,1)}, bf16[128,256]{1,0:T(8,128)(2,1)S(1)}, u32[]{:S(2)}, u32[]{:S(2)}) collective-permute-start(bf16[128,256]{1,0:T(8,128)(2,1)} %collective-permute-done.1), channel_id=1, source_target_pairs={{0,4},{4,8},{8,12},{12,0},{1,5},{5,9},{9,13},{13,1},{2,6},{6,10},{... | collective-permute-start | bytes 196616 | tf_op jit(solution)/shard_map/ppermute | solution.py:163
  183.4 1.0 copy-start.10
  (13 other events, 8.5 us)
